TPU v7x, 32 devices: a whole 2x2x4 slice. The times are simulated.
32 devices in a mesh: row: 8 (over z, y), col: 4 (over x, core).
Axes of the slice: x: 2, y: 2, z: 4, core: 2. Of those that a mesh axis runs over, the one named last changes fastest.
Arguments:
- tokens: bfloat16 [6272, 2048], P('row', 'col'), may hold values from -6 to 6
- first_gain: float32 [1024], P('col'), may hold values from 0.1 to 1.9
- first_shift: float32 [1024], P('col'), may hold values from -1.5 to 1.5
- inward_weight: bfloat16 [1024, 3, 1024], P('row', None, 'col'), may hold values from -0.25 to 0.25
- attention_bias: float32 [2, 1024], P(None, 'col'), may hold values from -2.5 to 2.5
- output_weight: bfloat16 [1024, 1024], P('col', 'row'), may hold values from -2 to 2
- output_bias: float32 [1024], P('col'), may hold values from -2.5 to 2.5
- second_gain: float32 [1024], P('col'), may hold values from 0.1 to 1.9
- second_shift: float32 [1024], P('col'), may hold values from -1.5 to 1.5
- expand_weight: bfloat16 [1024, 4096], P('row', 'col'), may hold values from -0.1875 to 0.1875
- expand_bias: float32 [4096], P('col'), may hold values from -2.5 to 2.5
- reduce_weight: bfloat16 [4096, 1024], P('col', 'row'), may hold values from -0.125 to 0.125
- reduce_bias: float32 [1024], P('col'), may hold values from -2.5 to 2.5
- cotangent: bfloat16 [6272, 2048], P('row', 'col'), may hold values from -6 to 6
Outputs:
- layer_output: bfloat16 [6272, 2048], P('row', 'col')
- tokens_grad: float32 [6272, 2048], P('row', 'col')
- first_gain_grad: float32 [1024], P('col')
- first_shift_grad: float32 [1024], P('col')
- inward_grad: float32 [1024, 3, 1024], P('row', None, 'col')
- attention_bias_grad: float32 [2, 1024], P(None, 'col')
- output_grad: float32 [1024, 1024], P('col', 'row')
- output_bias_grad: float32 [1024], P('col')
- second_gain_grad: float32 [1024], P('col')
- second_shift_grad: float32 [1024], P('col')
- expand_grad: float32 [1024, 4096], P('row', 'col')
- expand_bias_grad: float32 [4096], P('col')
- reduce_grad: float32 [4096, 1024], P('col', 'row')
- reduce_bias_grad: float32 [1024], P('col')
All inputs are finite; a program needn't handle non-finite values.
Results may differ from a plain program's by a relative error of at most 0.015.
The roundings to bfloat16 on the way count: a program that leaves them out, or rounds other values in their place, can miss the bound.
Values may be sent and summed in bfloat16 or wider, within the bound.
A program may use at most 192 MiB of HBM per device.

v0:
```python
import jax
import jax.numpy as jnp
from jax import lax
from jax.sharding import PartitionSpec as P

HEAD_DIM = 64
SEQ = 1568
EPSILON = 1e-06
CONTRACT_ROWS = (((0,), (0,)), ((), ()))
CONTRACT_COLS = (((1,), (1,)), ((), ()))


def norm_forward(values, gain, shift, full_width):
    row_total = lax.psum(jnp.sum(values, axis=1), "col")
    centred = values - (row_total / full_width)[:, None]
    row_square = lax.psum(jnp.sum(centred * centred, axis=1), "col")
    inverse = lax.rsqrt(row_square / full_width + EPSILON)
    unit_rows = centred * inverse[:, None]
    return (unit_rows, inverse, unit_rows * gain + shift)


def norm_backward(incoming, unit_rows, inverse, gain, full_width):
    scaled = incoming * gain
    plain_sum, cross_sum = lax.psum(
        (jnp.sum(scaled, axis=1), jnp.sum(scaled * unit_rows, axis=1)), "col"
    )
    result = inverse[:, None] * (
        scaled - (plain_sum / full_width)[:, None] - unit_rows * (cross_sum / full_width)[:, None]
    )
    return (result, jnp.sum(incoming * unit_rows, axis=0), jnp.sum(incoming, axis=0))


def spread_features(values):
    return lax.all_gather(values, "col", axis=1, tiled=True)


def sum_partials(values):
    return lax.psum_scatter(values, "col", scatter_dimension=1, tiled=True)


def spread_grads(values):
    return lax.all_gather(values, "col", axis=1, tiled=True)


def sum_grad_partials(values):
    return lax.psum_scatter(values, "col", scatter_dimension=1, tiled=True)


def fetch_weights(inward_weight, output_weight, expand_weight, reduce_weight):
    return (
        lax.all_gather(inward_weight, "row", axis=0, tiled=True),
        lax.all_gather(output_weight, "row", axis=1, tiled=True),
        lax.all_gather(expand_weight, "row", axis=0, tiled=True),
        lax.all_gather(reduce_weight, "row", axis=1, tiled=True),
    )


def attend_clip(queries, key_rows, value_rows, score_scale):
    seq_len = queries.shape[0]
    blocks = queries.reshape((2, seq_len // 2) + queries.shape[1:])

    def one_block(query_part):
        scores = (
            jnp.einsum("qhd,khd->hqk", query_part, key_rows, preferred_element_type=jnp.float32)
            * score_scale
        )
        row_peak = jnp.max(scores, axis=-1, keepdims=True)
        exponent = jnp.exp(scores - row_peak)
        row_sum = jnp.sum(exponent, axis=-1, keepdims=True)
        prob_low = (exponent / row_sum).astype(jnp.bfloat16)
        mixed_rows = jnp.einsum(
            "hqk,khd->qhd", prob_low, value_rows, preferred_element_type=jnp.float32
        )
        return (mixed_rows, (row_peak + jnp.log(row_sum))[..., 0])

    mixed_rows, logsum = lax.map(one_block, blocks)
    return (mixed_rows.reshape(queries.shape), logsum)


def attend_clip_back(queries, key_rows, value_rows, logsum, grad_out, score_scale):
    seq_len = queries.shape[0]
    block_shape = (2, seq_len // 2) + queries.shape[1:]

    def step_block(carry, pieces):
        key_acc, value_acc = carry
        query_part, grad_part, log_part = pieces
        scores = (
            jnp.einsum("qhd,khd->hqk", query_part, key_rows, preferred_element_type=jnp.float32)
            * score_scale
        )
        probs = jnp.exp(scores - log_part[..., None])
        grad_probs = jnp.einsum(
            "qhd,khd->hqk", grad_part, value_rows, preferred_element_type=jnp.float32
        )
        inner_sum = jnp.sum(probs * grad_probs, axis=-1, keepdims=True)
        grad_scores = (probs * (grad_probs - inner_sum)).astype(jnp.bfloat16)
        query_grad = (
            jnp.einsum("hqk,khd->qhd", grad_scores, key_rows, preferred_element_type=jnp.float32)
            * score_scale
        )
        key_acc = key_acc + jnp.einsum(
            "hqk,qhd->khd", grad_scores, query_part, preferred_element_type=jnp.float32
        )
        value_acc = value_acc + jnp.einsum(
            "hqk,qhd->khd",
            probs.astype(jnp.bfloat16),
            grad_part,
            preferred_element_type=jnp.float32,
        )
        return ((key_acc, value_acc), query_grad)

    zero_acc = jnp.zeros(key_rows.shape, jnp.float32)
    (key_acc, value_acc), query_grads = lax.scan(
        step_block,
        (zero_acc, zero_acc),
        (queries.reshape(block_shape), grad_out.reshape(block_shape), logsum),
    )
    return (query_grads.reshape(queries.shape), key_acc * score_scale, value_acc)


def forward_pass(
    tokens,
    first_gain,
    first_shift,
    attention_bias,
    output_bias,
    second_gain,
    second_shift,
    expand_bias,
    reduce_bias,
    gathered,
):
    inward_all, output_rows, expand_all, reduce_rows = gathered
    full_width = inward_all.shape[0]
    local_width = inward_all.shape[2]
    row_count = tokens.shape[0]
    clip_shape = (row_count // SEQ, SEQ, local_width // HEAD_DIM, HEAD_DIM)
    score_scale = HEAD_DIM ** (-0.5)
    source = tokens.astype(jnp.float32)
    unit_one, inverse_one, normed_one = norm_forward(source, first_gain, first_shift, full_width)
    normed_all = spread_features(normed_one.astype(jnp.bfloat16))
    projected = jnp.dot(
        normed_all,
        inward_all.reshape(full_width, 3 * local_width),
        preferred_element_type=jnp.float32,
    )
    projected = projected.reshape(row_count, 3, local_width)
    queries = (projected[:, 0] + attention_bias[0]).astype(jnp.bfloat16)
    key_rows = projected[:, 1].astype(jnp.bfloat16)
    value_rows = (projected[:, 2] + attention_bias[1]).astype(jnp.bfloat16)
    mixed_rows, logsum = lax.map(
        lambda clip_parts: attend_clip(clip_parts[0], clip_parts[1], clip_parts[2], score_scale),
        (queries.reshape(clip_shape), key_rows.reshape(clip_shape), value_rows.reshape(clip_shape)),
    )
    mixed_low = mixed_rows.reshape(row_count, local_width).astype(jnp.bfloat16)
    hidden_state = (
        source
        + sum_partials(jnp.dot(mixed_low, output_rows, preferred_element_type=jnp.float32))
        + output_bias
    )
    unit_two, inverse_two, normed_two = norm_forward(
        hidden_state, second_gain, second_shift, full_width
    )
    normed_all_two = spread_features(normed_two.astype(jnp.bfloat16))
    expanded = jnp.dot(normed_all_two, expand_all, preferred_element_type=jnp.float32) + expand_bias
    activated = jax.nn.gelu(expanded, approximate=False).astype(jnp.bfloat16)
    output_value = (
        hidden_state
        + sum_partials(jnp.dot(activated, reduce_rows, preferred_element_type=jnp.float32))
        + reduce_bias
    )
    saved_state = (
        unit_one,
        inverse_one,
        normed_all,
        queries,
        key_rows,
        value_rows,
        logsum,
        mixed_low,
        unit_two,
        inverse_two,
        normed_all_two,
        expanded,
        activated,
    )
    return (output_value, saved_state)


def per_device(
    tokens,
    first_gain,
    first_shift,
    inward_weight,
    attention_bias,
    output_weight,
    output_bias,
    second_gain,
    second_shift,
    expand_weight,
    expand_bias,
    reduce_weight,
    reduce_bias,
    cotangent,
):
    packed_width = tokens.shape[1]
    tokens = tokens.reshape(-1, packed_width // 2)
    cotangent = cotangent.reshape(-1, packed_width // 2)
    gathered = fetch_weights(inward_weight, output_weight, expand_weight, reduce_weight)
    output_value, saved_state = forward_pass(
        tokens,
        first_gain,
        first_shift,
        attention_bias,
        output_bias,
        second_gain,
        second_shift,
        expand_bias,
        reduce_bias,
        gathered,
    )
    gathered = fetch_weights(inward_weight, output_weight, expand_weight, reduce_weight)
    unused_value, saved_state = forward_pass(
        tokens,
        first_gain,
        first_shift,
        attention_bias,
        output_bias,
        second_gain,
        second_shift,
        expand_bias,
        reduce_bias,
        gathered,
    )
    inward_all, output_rows, expand_all, reduce_rows = gathered
    (
        unit_one,
        inverse_one,
        normed_all,
        queries,
        key_rows,
        value_rows,
        logsum,
        mixed_low,
        unit_two,
        inverse_two,
        normed_all_two,
        expanded,
        activated,
    ) = saved_state
    full_width = inward_all.shape[0]
    local_width = inward_all.shape[2]
    row_count = tokens.shape[0]
    clip_shape = (row_count // SEQ, SEQ, local_width // HEAD_DIM, HEAD_DIM)
    score_scale = HEAD_DIM ** (-0.5)
    grad_rows = cotangent.astype(jnp.float32)
    grad_all = spread_grads(cotangent)
    grad_act = lax.dot_general(
        grad_all, reduce_rows, CONTRACT_COLS, preferred_element_type=jnp.float32
    )
    reduce_grad = lax.dot_general(
        activated, grad_all, CONTRACT_ROWS, preferred_element_type=jnp.float32
    )
    reduce_bias_grad = jnp.sum(grad_rows, axis=0)
    gelu_value, gelu_back = jax.vjp(
        lambda inner_value: jax.nn.gelu(inner_value, approximate=False), expanded
    )
    grad_expanded = gelu_back(grad_act)[0].astype(jnp.bfloat16)
    expand_grad = lax.dot_general(
        normed_all_two, grad_expanded, CONTRACT_ROWS, preferred_element_type=jnp.float32
    )
    expand_bias_grad = jnp.sum(grad_expanded.astype(jnp.float32), axis=0)
    grad_normed_two = sum_grad_partials(
        lax.dot_general(
            grad_expanded, expand_all, CONTRACT_COLS, preferred_element_type=jnp.float32
        )
    )
    back_two, second_gain_grad, second_shift_grad = norm_backward(
        grad_normed_two, unit_two, inverse_two, second_gain, full_width
    )
    grad_hidden = grad_rows + back_two
    grad_hidden_low = grad_hidden.astype(jnp.bfloat16)
    grad_hidden_all = spread_grads(grad_hidden_low)
    output_grad = lax.dot_general(
        mixed_low, grad_hidden_all, CONTRACT_ROWS, preferred_element_type=jnp.float32
    )
    output_bias_grad = jnp.sum(grad_hidden_low.astype(jnp.float32), axis=0)
    grad_mixed = lax.dot_general(
        grad_hidden_all, output_rows, CONTRACT_COLS, preferred_element_type=jnp.float32
    ).astype(jnp.bfloat16)
    query_grads, key_grads, value_grads = lax.map(
        lambda clip_parts: attend_clip_back(
            clip_parts[0], clip_parts[1], clip_parts[2], clip_parts[3], clip_parts[4], score_scale
        ),
        (
            queries.reshape(clip_shape),
            key_rows.reshape(clip_shape),
            value_rows.reshape(clip_shape),
            logsum,
            grad_mixed.reshape(clip_shape),
        ),
    )
    stacked = jnp.stack(
        [
            query_grads.reshape(row_count, local_width),
            key_grads.reshape(row_count, local_width),
            value_grads.reshape(row_count, local_width),
        ],
        axis=1,
    ).astype(jnp.bfloat16)
    attention_bias_grad = jnp.stack(
        [
            jnp.sum(stacked[:, 0].astype(jnp.float32), axis=0),
            jnp.sum(stacked[:, 2].astype(jnp.float32), axis=0),
        ]
    )
    flat_grads = stacked.reshape(row_count, 3 * local_width)
    inward_grad = lax.dot_general(
        normed_all, flat_grads, CONTRACT_ROWS, preferred_element_type=jnp.float32
    ).reshape(full_width, 3, local_width)
    grad_normed_one = sum_grad_partials(
        lax.dot_general(
            flat_grads,
            inward_all.reshape(full_width, 3 * local_width),
            CONTRACT_COLS,
            preferred_element_type=jnp.float32,
        )
    )
    back_one, first_gain_grad, first_shift_grad = norm_backward(
        grad_normed_one, unit_one, inverse_one, first_gain, full_width
    )
    tokens_grad = grad_hidden + back_one
    inward_grad, output_grad, expand_grad, reduce_grad = (
        lax.psum_scatter(
            inward_grad.astype(jnp.bfloat16), "row", scatter_dimension=0, tiled=True
        ).astype(jnp.float32),
        lax.psum_scatter(
            output_grad.astype(jnp.bfloat16), "row", scatter_dimension=1, tiled=True
        ).astype(jnp.float32),
        lax.psum_scatter(
            expand_grad.astype(jnp.bfloat16), "row", scatter_dimension=0, tiled=True
        ).astype(jnp.float32),
        lax.psum_scatter(
            reduce_grad.astype(jnp.bfloat16), "row", scatter_dimension=1, tiled=True
        ).astype(jnp.float32),
    )
    (
        first_gain_grad,
        first_shift_grad,
        attention_bias_grad,
        output_bias_grad,
        second_gain_grad,
        second_shift_grad,
        expand_bias_grad,
        reduce_bias_grad,
    ) = lax.psum(
        (
            first_gain_grad,
            first_shift_grad,
            attention_bias_grad,
            output_bias_grad,
            second_gain_grad,
            second_shift_grad,
            expand_bias_grad,
            reduce_bias_grad,
        ),
        "row",
    )
    return (
        output_value.astype(jnp.bfloat16).reshape(-1, packed_width),
        tokens_grad.reshape(-1, packed_width),
        first_gain_grad,
        first_shift_grad,
        inward_grad,
        attention_bias_grad,
        output_grad,
        output_bias_grad,
        second_gain_grad,
        second_shift_grad,
        expand_grad,
        expand_bias_grad,
        reduce_grad,
        reduce_bias_grad,
    )


def solution(mesh):
    in_specs = (
        P("row", "col"),
        P("col"),
        P("col"),
        P("row", None, "col"),
        P(None, "col"),
        P("col", "row"),
        P("col"),
        P("col"),
        P("col"),
        P("row", "col"),
        P("col"),
        P("col", "row"),
        P("col"),
        P("row", "col"),
    )
    out_specs = (
        P("row", "col"),
        P("row", "col"),
        P("col"),
        P("col"),
        P("row", None, "col"),
        P(None, "col"),
        P("col", "row"),
        P("col"),
        P("col"),
        P("col"),
        P("row", "col"),
        P("col"),
        P("col", "row"),
        P("col"),
    )
    return jax.shard_map(
        per_device, mesh=mesh, in_specs=in_specs, out_specs=out_specs, check_vma=False
    )
```

profile of v0, /device:TPU:0, one launch (start us, length us, event | category | flops | bytes accessed | tf_op | source)
XLA Modules:
  0.0 1172.3 jit_solution(17945256681787545454)
XLA Ops:
  9.6 8.5 psum.132
  18.7 5.9 psum.133
  27.5 32.0 %all_gather.34 = bf16[256,1024]{1,0:T(8,128)(2,1)} all-gather(bf16[256,128]{1,0:T(8,128)(2,1)S(1)} %copy-done.18), channel_id=1, replica_groups=mesh['row'=8,'col'=4] {'row'}, dimensions={1}, use_global_device_ids=true | all-gather | bytes 589824 | tf_op jit(solution)/shard_map/all_gather | solution.py:52
  63.6 29.1 %all-gather.9.cloned.1.call-done = bf16[1568,1024]{1,0:T(8,128)(2,1)} async-done(((bf16[1568,256]{1,0:T(8,128)(2,1)}), bf16[1568,1024]{1,0:T(8,128)(2,1)}) %all-gather.9.cloned.1.call-update) | async-done | bytes 3211280 | tf_op jit(solution)/shard_map/all_gather | solution.py:34
  109.3 34.0 %while.64 = (s32[]{:T(128)}, bf16[2,784,4,64]{1,3,2,0:T(8,128)(2,1)S(1)}, bf16[2,784,4,64]{1,3,2,0:T(8,128)(2,1)}, bf16[1568,4,64]{0,2,1:T(8,128)(2,1)}, bf16[1568,4,64]{0,2,1:T(8,128)(2,1)}, /*index=5*/s32[]{:T(128)}) while((s32[]{:T(128)}, bf16[2,784,4,64]{1,3,2,0:T(8,128)(2,1)S(1)}, bf16[2,784,4,64]{1,3,2,0:T(8,128)(2,1)}, ...), condition=%wide.region_7.0_spmd, body=%wide.region_4.7_spmd.sunk | while | flops 1922650112 | bytes 4304209 | solution.py:76
  109.5 7.7 fusion.207
  117.2 9.0 fusion.208
  126.3 7.7 fusion.207
  134.0 9.0 fusion.208
  149.7 30.1 %while.65 = (s32[]{:T(128)}, bf16[2,784,4,64]{1,3,2,0:T(8,128)(2,1)}, f32[2,4,784]{2,1,0:T(4,128)S(1)}, bf16[2,784,4,64]{1,3,2,0:T(8,128)(2,1)}, bf16[1568,4,64]...) while((s32[]{:T(128)}, bf16[2,784,4,64]{1,3,2,0:T(8,128)(2,1)}, ...), condition=%wide.region_17.18_spmd, body=%wide.region_14.17_spmd.sunk | while | flops 1303067648 | bytes 62078304 | solution.py:76
  158.1 6.7 fusion.212
  173.2 6.6 fusion.212
  188.3 19.6 %reduce-scatter.14.cloned.1.call-done = f32[1568,256]{1,0:T(8,128)} async-done(((f32[1568,1024]{1,0:T(8,128)}), f32[1568,256]{1,0:T(8,128)}) %reduce-scatter.14.cloned.1.call-update) | async-done | bytes 1605648 | tf_op jit(solution)/shard_map/reduce_scatter | solution.py:38
  207.9 61.8 %reduce-scatter.18.cloned.1.call-done = f32[1568,256]{1,0:T(8,128)} async-done(((f32[1568,1024]{1,0:T(8,128)}), f32[1568,256]{1,0:T(8,128)}) %reduce-scatter.18.cloned.1.call-update) | async-done | bytes 1605648 | tf_op jit(solution)/shard_map/reduce_scatter | solution.py:38
  273.3 6.3 psum.136
  280.2 6.2 psum.137
  290.8 30.3 %all-gather.15.cloned.1.call-done = bf16[1024,1024]{1,0:T(8,128)(2,1)} async-done(((bf16[128,1024]{1,0:T(8,128)(2,1)}), bf16[1024,1024]{1,0:T(8,128)(2,1)}) %all-gather.15.cloned.1.call-update) | async-done | bytes 2097168 | tf_op jit(solution)/shard_map/all_gather | solution.py:53
  321.1 29.8 %all-gather.19.cloned.1.call-done = bf16[1568,1024]{1,0:T(8,128)(2,1)} async-done(((bf16[1568,256]{1,0:T(8,128)(2,1)}), bf16[1568,1024]{1,0:T(8,128)(2,1)}) %all-gather.19.cloned.1.call-update) | async-done | bytes 3211280 | tf_op jit(solution)/shard_map/all_gather | solution.py:34
  350.9 8.7 fusion.142
  359.6 44.5 %all-gather.17.cloned.1.call-done = bf16[1024,1024]{1,0:T(8,128)(2,1)} async-done(((bf16[1024,128]{1,0:T(8,128)(2,1)}), bf16[1024,1024]{1,0:T(8,128)(2,1)}) %all-gather.17.cloned.1.call-update) | async-done | bytes 2097168 | tf_op jit(solution)/shard_map/all_gather | solution.py:54
  404.1 29.1 %all-gather.21.cloned.1.call-done = bf16[1568,1024]{1,0:T(8,128)(2,1)} async-done(((bf16[1568,256]{1,0:T(8,128)(2,1)}), bf16[1568,1024]{1,0:T(8,128)(2,1)}) %all-gather.21.cloned.1.call-update) | async-done | bytes 3211280 | tf_op jit(solution)/shard_map/all_gather | solution.py:42
  433.1 22.4 %convert_reduce_fusion = (f32[1024]{0:T(1024)}, bf16[1568,1024]{1,0:T(8,128)(2,1)S(1)}, f32[1568,1024]{1,0:T(8,128)}) fusion(f32[1568,1024]{1,0:T(8,128)} %fusion.142, f32[1024]{0:T(1024)S(1)} %copy-done.34, bf16[1568,1024]{1,0:T(8,128)(2,1)} %all-gather.21.cloned.1.call-done, bf16[1024,1024]{1,0:T(8,128)(2,1)} %all-gather.17.cloned.1.call-done), kind=kOutput, calls=%fused_computation.69 | convolution fusion | flops 3408755712 | bytes 21372928 | tf_op jit(solution)/shard_map/dot_general | solution.py:258
  457.2 5.5 fusion.143
  463.0 59.1 %reduce-scatter.20.cloned.1.call-done = f32[1568,256]{1,0:T(8,128)} async-done(((f32[1568,1024]{1,0:T(8,128)}), f32[1568,256]{1,0:T(8,128)}) %reduce-scatter.20.cloned.1.call-update) | async-done | bytes 1605648 | tf_op jit(solution)/shard_map/reduce_scatter | solution.py:46
  525.1 10.3 all-reduce.2
  539.3 31.0 %all-gather.23.cloned.1.call-done = bf16[1568,1024]{1,0:T(8,128)(2,1)} async-done(((bf16[1568,256]{1,0:T(8,128)(2,1)}), bf16[1568,1024]{1,0:T(8,128)(2,1)}) %all-gather.23.cloned.1.call-update) | async-done | bytes 3211280 | tf_op jit(solution)/shard_map/all_gather | solution.py:42
  578.0 129.4 %while.66 = (s32[]{:T(128)}, f32[1568,4,64]{0,2,1:T(8,128)}, f32[1568,4,64]{0,2,1:T(8,128)}, bf16[2,784,4,64]{1,3,2,0:T(8,128)(2,1)}, bf16[2,784,4,64]{1,3,2,0:T...) while((s32[]{:T(128)}, f32[1568,4,64]{0,2,1:T(8,128)}, ...), condition=%wide.region_30.31_spmd.clone, body=%wide.region_28.30_spmd.clone.sunk | while | flops 3188179968 | bytes 291960320 | solution.py:113
  578.0 11.2 fusion.222
  589.1 13.9 %multiply_reduce_fusion.15 = (f32[4,784]{1,0:T(4,128)S(1)}, f32[4,784,1568]{2,1,0:T(8,128)}) fusion(f32[4,784,1568]{2,1,0:T(8,128)} %fusion.222, f32[4,784]{1,0:T(4,128)S(1)} %dynamic-slice_bitcast_fusion.2, bf16[1568,4,64]{0,2,1:T(8,128)(2,1)} %get-tuple-element.563, bf16[2,784,4,64]{1,3,2,0:T(8,128)(2,1)} %get-tuple-element.562, s32[]{:T(128)S(6)} %copy.105), kind=kOutput, calls=%fused_computation.37.clone.1 | convolution fusion | flops 649073600 | bytes 41878020 | tf_op jit(solution)/shard_map/while/body/eval_jaxpr/while/body/eval_jaxpr/qhd,khd->hqk/dot_general | solution.py:88
  603.0 18.2 %multiply_convert_fusion.6 = bf16[4,784,1568]{2,1,0:T(8,128)(2,1)} fusion(f32[4,784,1568]{2,1,0:T(8,128)} %get-tuple-element.495, f32[4,784,1568]{2,1,0:T(8,128)} %fusion.222, f32[4,784]{1,0:T(4,128)S(1)} %get-tuple-element.496), kind=kLoop, calls=%fused_computation.36.clone.1 | loop fusion | flops 14751744 | bytes 49185024 | tf_op jit(solution)/shard_map/while/body/eval_jaxpr/while/body/eval_jaxpr/convert_element_type | solution.py:96
  629.8 8.3 fusion.225
  642.4 11.1 fusion.222
  653.5 13.9 %multiply_reduce_fusion.15 = (f32[4,784]{1,0:T(4,128)S(1)}, f32[4,784,1568]{2,1,0:T(8,128)}) fusion(f32[4,784,1568]{2,1,0:T(8,128)} %fusion.222, f32[4,784]{1,0:T(4,128)S(1)} %dynamic-slice_bitcast_fusion.2, bf16[1568,4,64]{0,2,1:T(8,128)(2,1)} %get-tuple-element.563, bf16[2,784,4,64]{1,3,2,0:T(8,128)(2,1)} %get-tuple-element.562, s32[]{:T(128)S(6)} %copy.105), kind=kOutput, calls=%fused_computation.37.clone.1 | convolution fusion | flops 649073600 | bytes 41878020 | tf_op jit(solution)/shard_map/while/body/eval_jaxpr/while/body/eval_jaxpr/qhd,khd->hqk/dot_general | solution.py:88
  667.4 18.2 %multiply_convert_fusion.6 = bf16[4,784,1568]{2,1,0:T(8,128)(2,1)} fusion(f32[4,784,1568]{2,1,0:T(8,128)} %get-tuple-element.495, f32[4,784,1568]{2,1,0:T(8,128)} %fusion.222, f32[4,784]{1,0:T(4,128)S(1)} %get-tuple-element.496), kind=kLoop, calls=%fused_computation.36.clone.1 | loop fusion | flops 14751744 | bytes 49185024 | tf_op jit(solution)/shard_map/while/body/eval_jaxpr/while/body/eval_jaxpr/convert_element_type | solution.py:96
  694.7 8.3 fusion.225
  718.0 6.0 convolution_bitcast_fusion.1
  726.0 57.5 %reduce-scatter.22.cloned.1.call-done = f32[1568,256]{1,0:T(8,128)} async-done(((f32[1568,1024]{1,0:T(8,128)}), f32[1568,256]{1,0:T(8,128)}) %reduce-scatter.22.cloned.1.call-update) | async-done | bytes 1605648 | tf_op jit(solution)/shard_map/reduce_scatter | solution.py:46
  785.9 10.3 all-reduce.1
  797.6 11.4 fusion.95
  813.5 8.3 convolution_convert_fusion.1
  828.2 6.9 fusion.96
  835.3 23.6 %fusion.94 = f32[1568,1024]{1,0:T(8,128)} fusion(bf16[1024,1024]{1,0:T(8,128)(2,1)} %all-gather.17.cloned.1.call-done, bf16[1568,1024]{1,0:T(8,128)(2,1)} %all-gather.13.cloned.1.call-done, bf16[1024,1024]{1,0:T(8,128)(2,1)} %all-gather.15.cloned.1.call-done, f32[1024]{0:T(1024)S(1)} %copy-done.35), kind=kOutput, calls=%fused_computation.110 | convolution fusion | flops 6682640384 | bytes 13832192 | tf_op jit(solution)/shard_map/dot_general | solution.py:169
  858.9 40.4 %reduce-scatter.30.cloned.1.call-done = bf16[128,1024]{1,0:T(8,128)(2,1)} async-done(((bf16[1024,1024]{1,0:T(8,128)(2,1)}), bf16[128,1024]{1,0:T(8,128)(2,1)}) %reduce-scatter.30.cloned.1.call-update) | async-done | bytes 262160
  901.3 68.0 %reduce-scatter.26.cloned.1.call-done = bf16[128,1024]{1,0:T(8,128)(2,1)} async-done(((bf16[1024,1024]{1,0:T(8,128)(2,1)}), bf16[128,1024]{1,0:T(8,128)(2,1)}) %reduce-scatter.26.cloned.1.call-update) | async-done | bytes 262160 | tf_op jit(solution)/shard_map/reduce_scatter | solution.py:340
  972.8 60.7 %reduce-scatter.28.cloned.1.call-done = bf16[128,256]{1,0:T(8,128)(2,1)} async-done(((bf16[1024,256]{1,0:T(8,128)(2,1)}), bf16[128,256]{1,0:T(8,128)(2,1)}) %reduce-scatter.28.cloned.1.call-update) | async-done | bytes 65552
  1035.1 67.1 %reduce-scatter.24.cloned.1.call-done = bf16[128,3,256]{2,0,1:T(8,128)(2,1)} async-done(((bf16[1024,3,256]{2,0,1:T(8,128)(2,1)}), bf16[128,3,256]{2,0,1:T(8,128)(2,1)}) %reduce-scatter.24.cloned.1.call-update) | async-done | bytes 196624 | tf_op jit(solution)/shard_map/reduce_scatter | solution.py:334
  1110.1 35.1 %all-reduce = (f32[256]{0:T(256)}, f32[256]{0:T(256)}, f32[2,256]{1,0:T(2,128)}, f32[256]{0:T(256)}, f32[256]{0:T(256)}, /*index=5*/f32[256]{0:T(256)}, f32[1024]{0:T(1024)}, f32[256]{0:T(256)}) all-reduce(f32[256]{0:T(256)S(1)} %get-tuple-element.281, f32[256]{0:T(256)S(1)} %get-tuple-element.288, ...), channel_id=1, replica_groups=mesh['row'=8,'col'=4] {'row'}, use_global_device_ids=true, to_apply=%region_37.38 | all-reduce | flops 3072 | bytes 24576 | tf_op jit(solution)/shard_map/psum | solution.py:356
  1145.2 17.6 %reduce-scatter.16.cloned.1.call-done = f32[1568,256]{1,0:T(8,128)} async-done(((f32[1568,1024]{1,0:T(8,128)}), f32[1568,256]{1,0:T(8,128)}) %reduce-scatter.16.cloned.1.call-update) | async-done | bytes 1605648 | tf_op jit(solution)/shard_map/reduce_scatter | solution.py:38
  (202 shorter events, 154.4 us)
Async XLA Ops:
  7.2 20.1 %copy-start.30 = (f32[2,256]{1,0:T(2,128)S(1)}, f32[2,256]{1,0:T(2,128)}, u32[]{:S(2)}) copy-start(f32[2,256]{1,0:T(2,128)} %param.24) | copy-start | bytes 6148
  7.2 20.3 %copy-start.18 = (bf16[256,128]{1,0:T(8,128)(2,1)S(1)}, bf16[256,128]{1,0:T(8,128)(2,1)}, u32[]{:S(2)}) copy-start(bf16[256,128]{1,0:T(8,128)(2,1)} %param.25) | copy-start | bytes 196612
  7.2 54.7 %all-gather.11.cloned.1.call-start = ((), (), s32[]{:S(2)}) async-start(), calls=%async_computation.10 | async-start | bytes 1769472 | tf_op jit(solution)/shard_map/all_gather | solution.py:51
  7.9 84.8 %all-gather.9.cloned.1.call-start = ((), (), s32[]{:S(2)}) async-start(), calls=%async_computation.9 | async-start | bytes 4014080 | tf_op jit(solution)/shard_map/all_gather | solution.py:34
  9.3 88.1 %copy-start.2 = (f32[1568,256]{1,0:T(8,128)}, f32[1568,256]{1,0:T(8,128)S(1)}, u32[]{:S(2)}) copy-start(f32[1568,256]{1,0:T(8,128)S(1)} %reshape.165) | copy-start | bytes 4816900
  18.1 41.3 %copy-start.14 = (f32[1568]{0:T(1024)}, f32[1568]{0:T(1024)S(1)}, u32[]{:S(2)}) copy-start(f32[1568]{0:T(1024)S(1)} %broadcast_multiply_fusion.7) | copy-start | bytes 18820
  27.2 180.7 %reduce-scatter.14.cloned.1.call-start = ((), (), s32[]{:S(2)}) async-start(), calls=%async_computation.11 | async-start | bytes 8028160 | tf_op jit(solution)/shard_map/reduce_scatter | solution.py:38
  109.3 35.5 %copy-start.12 = (bf16[256,1024]{1,0:T(8,128)(2,1)S(1)}, bf16[256,1024]{1,0:T(8,128)(2,1)}, u32[]{:S(2)}) copy-start(bf16[256,1024]{1,0:T(8,128)(2,1)} %all_gather.34) | copy-start | bytes 1572868
  148.6 121.2 %reduce-scatter.18.cloned.1.call-start = ((), (), s32[]{:S(2)}) async-start(), calls=%async_computation.16 | async-start | bytes 8028160 | tf_op jit(solution)/shard_map/reduce_scatter | solution.py:38
  182.5 87.3 %copy-start.3 = (f32[1568,256]{1,0:T(8,128)S(1)}, f32[1568,256]{1,0:T(8,128)}, u32[]{:S(2)}) copy-start(f32[1568,256]{1,0:T(8,128)} %copy-done.2) | copy-start | bytes 4816900
  182.5 87.3 %copy-start.31 = (f32[256]{0:T(256)S(1)}, f32[256]{0:T(256)}, u32[]{:S(2)}) copy-start(f32[256]{0:T(256)} %param.26) | copy-start | bytes 3076
  187.7 98.7 %copy-start.19 = (f32[256]{0:T(256)S(1)}, f32[256]{0:T(256)}, u32[]{:S(2)}) copy-start(f32[256]{0:T(256)} %param.27) | copy-start | bytes 3076
  187.7 98.7 %copy-start.23 = (f32[256]{0:T(256)S(1)}, f32[256]{0:T(256)}, u32[]{:S(2)}) copy-start(f32[256]{0:T(256)} %param.28) | copy-start | bytes 3076
  187.7 133.4 %all-gather.15.cloned.1.call-start = ((), (), s32[]{:S(2)}) async-start(), calls=%async_computation.13 | async-start | bytes 2359296 | tf_op jit(solution)/shard_map/all_gather | solution.py:53
  188.3 162.6 %all-gather.19.cloned.1.call-start = ((), (), s32[]{:S(2)}) async-start(), calls=%async_computation.17 | async-start | bytes 4014080 | tf_op jit(solution)/shard_map/all_gather | solution.py:34
  287.8 116.3 %all-gather.17.cloned.1.call-start = ((), (), s32[]{:S(2)}) async-start(), calls=%async_computation.14 | async-start | bytes 2359296 | tf_op jit(solution)/shard_map/all_gather | solution.py:54
  288.5 144.6 %all-gather.21.cloned.1.call-start = ((), (), s32[]{:S(2)}) async-start(), calls=%async_computation.18 | async-start | bytes 4014080 | tf_op jit(solution)/shard_map/all_gather | solution.py:42
  290.7 142.4 %copy-start.34 = (f32[1024]{0:T(1024)S(1)}, f32[1024]{0:T(1024)}, u32[]{:S(2)}) copy-start(f32[1024]{0:T(1024)} %param.30) | copy-start | bytes 12292
  290.7 231.4 %reduce-scatter.20.cloned.1.call-start = ((), (), s32[]{:S(2)}) async-start(), calls=%async_computation.19 | async-start | bytes 8028160 | tf_op jit(solution)/shard_map/reduce_scatter | solution.py:46
  433.1 24.1 %copy-start.33 = (bf16[1024,1024]{1,0:T(8,128)(2,1)S(1)}, bf16[1024,1024]{1,0:T(8,128)(2,1)}, u32[]{:S(2)}) copy-start(bf16[1024,1024]{1,0:T(8,128)(2,1)} %all-gather.15.cloned.1.call-done) | copy-start | bytes 6291460
  462.7 72.6 %copy-start.9 = (bf16[1568,256]{1,0:T(8,128)(2,1)S(1)}, bf16[1568,256]{1,0:T(8,128)(2,1)}, u32[]{:S(2)}) copy-start(bf16[1568,256]{1,0:T(8,128)(2,1)} %reshape.162) | copy-start | bytes 2408452
  462.7 107.6 %copy-start.13 = (bf16[256,1024]{1,0:T(8,128)(2,1)S(1)}, bf16[256,1024]{1,0:T(8,128)(2,1)}, u32[]{:S(2)}) copy-start(bf16[256,1024]{1,0:T(8,128)(2,1)} %all_gather.34) | copy-start | bytes 1572868
  462.7 107.6 %all-gather.23.cloned.1.call-start = ((), (), s32[]{:S(2)}) async-start(), calls=%async_computation.20 | async-start | bytes 4014080 | tf_op jit(solution)/shard_map/all_gather | solution.py:42
  539.2 244.2 %reduce-scatter.22.cloned.1.call-start = ((), (), s32[]{:S(2)}) async-start(), calls=%async_computation.21 | async-start | bytes 8028160 | tf_op jit(solution)/shard_map/reduce_scatter | solution.py:46
  603.0 22.7 %copy-start = (f32[4,784,1568]{2,1,0:T(8,128)S(1)}, f32[4,784,1568]{2,1,0:T(8,128)}, u32[]{:S(2)}) copy-start(f32[4,784,1568]{2,1,0:T(8,128)} %get-tuple-element.495) | copy-start | bytes 59006980 | tf_op jit(solution)/shard_map/while/body/eval_jaxpr/while
  629.8 8.3 copy-start.1
  629.8 8.3 copy-start.5
  667.4 22.7 %copy-start = (f32[4,784,1568]{2,1,0:T(8,128)S(1)}, f32[4,784,1568]{2,1,0:T(8,128)}, u32[]{:S(2)}) copy-start(f32[4,784,1568]{2,1,0:T(8,128)} %get-tuple-element.495) | copy-start | bytes 59006980 | tf_op jit(solution)/shard_map/while/body/eval_jaxpr/while
  694.7 8.3 copy-start.5
  724.0 59.5 %copy-start.4 = (f32[1568,256]{1,0:T(8,128)S(1)}, f32[1568,256]{1,0:T(8,128)}, u32[]{:S(2)}) copy-start(f32[1568,256]{1,0:T(8,128)} %copy-done.2) | copy-start | bytes 4816900
  724.0 59.5 %copy-start.15 = (f32[1568]{0:T(1024)S(1)}, f32[1568]{0:T(1024)}, u32[]{:S(2)}) copy-start(f32[1568]{0:T(1024)} %copy-done.14) | copy-start | bytes 18820
  724.0 59.5 %copy-start.17 = (f32[1568]{0:T(1024)S(1)}, f32[1568]{0:T(1024)}, u32[]{:S(2)}) copy-start(f32[1568]{0:T(1024)} %copy-done.16) | copy-start | bytes 18820
  724.0 59.5 %copy-start.21 = (f32[256]{0:T(256)S(1)}, f32[256]{0:T(256)}, u32[]{:S(2)}) copy-start(f32[256]{0:T(256)} %param.21) | copy-start | bytes 3076
  724.1 72.1 %copy-start.20 = (f32[256]{0:T(256)S(1)}, f32[256]{0:T(256)}, u32[]{:S(2)}) copy-start(f32[256]{0:T(256)} %param.27) | copy-start | bytes 3076
  724.1 72.1 %copy-start.24 = (f32[256]{0:T(256)S(1)}, f32[256]{0:T(256)}, u32[]{:S(2)}) copy-start(f32[256]{0:T(256)} %param.28) | copy-start | bytes 3076
  724.1 73.6 %copy-start.35 = (f32[1024]{0:T(1024)S(1)}, f32[1024]{0:T(1024)}, u32[]{:S(2)}) copy-start(f32[1024]{0:T(1024)} %param.30) | copy-start | bytes 12292
  724.1 111.2 %all-gather.13.cloned.1.call-start = ((), (), s32[]{:S(2)}) async-start(), calls=%async_computation.12 | async-start | bytes 4014080 | tf_op jit(solution)/shard_map/all_gather | solution.py:34
  797.6 101.7 %reduce-scatter.30.cloned.1.call-start = ((), (), s32[]{:S(2)}) async-start(), calls=%async_computation.25 | async-start | bytes 2359296
  813.1 156.3 %reduce-scatter.26.cloned.1.call-start = ((), (), s32[]{:S(2)}) async-start(), calls=%async_computation.23 | async-start | bytes 2359296 | tf_op jit(solution)/shard_map/reduce_scatter | solution.py:340
  821.9 211.6 %reduce-scatter.28.cloned.1.call-start = ((), (), s32[]{:S(2)}) async-start(), calls=%async_computation.24 | async-start | bytes 589824
  828.1 274.1 %reduce-scatter.24.cloned.1.call-start = ((), (), s32[]{:S(2)}) async-start(), calls=%async_computation.22 | async-start | bytes 1769472 | tf_op jit(solution)/shard_map/reduce_scatter | solution.py:334
  835.1 327.7 %reduce-scatter.16.cloned.1.call-start = ((), (), s32[]{:S(2)}) async-start(), calls=%async_computation.15 | async-start | bytes 8028160 | tf_op jit(solution)/shard_map/reduce_scatter | solution.py:38
  901.3 208.8 %copy-start.25 = (f32[256]{0:T(256)S(1)}, f32[256]{0:T(256)}, u32[]{:S(2)}) copy-start(f32[256]{0:T(256)} %get-tuple-element.279) | copy-start | bytes 3076
  901.3 208.8 %copy-start.26 = (f32[256]{0:T(256)S(1)}, f32[256]{0:T(256)}, u32[]{:S(2)}) copy-start(f32[256]{0:T(256)} %get-tuple-element.287) | copy-start | bytes 3076
  901.3 208.8 %copy-start.27 = (f32[256]{0:T(256)S(1)}, f32[256]{0:T(256)}, u32[]{:S(2)}) copy-start(f32[256]{0:T(256)} %get-tuple-element.348) | copy-start | bytes 3076
  901.3 208.8 %copy-start.28 = (f32[256]{0:T(256)S(1)}, f32[256]{0:T(256)}, u32[]{:S(2)}) copy-start(f32[256]{0:T(256)} %get-tuple-element.363) | copy-start | bytes 3076
  901.3 208.8 %copy-start.29 = (f32[1024]{0:T(1024)S(1)}, f32[1024]{0:T(1024)}, u32[]{:S(2)}) copy-start(f32[1024]{0:T(1024)} %get-tuple-element.345) | copy-start | bytes 12292
  901.3 261.5 %copy-start.32 = (f32[256]{0:T(256)S(1)}, f32[256]{0:T(256)}, u32[]{:S(2)}) copy-start(f32[256]{0:T(256)} %param.32) | copy-start | bytes 3076
  (10 other events, 28.9 us)
Sparse Core Ops, SparseCore 0:
  10.2 51.6 all-gather.10
  64.0 28.6 all-gather.8
  148.7 59.2 reduce-scatter.13
  210.5 59.2 reduce-scatter.17
  271.8 49.2 all-gather.14
  323.1 27.7 all-gather.18
  352.9 51.0 all-gather.16
  405.6 27.4 all-gather.20
  462.9 59.2 reduce-scatter.19
  539.4 30.9 all-gather.22
  724.2 59.2 reduce-scatter.21
  797.7 30.3 all-gather.12
  831.6 67.6 reduce-scatter.29
  902.7 66.6 reduce-scatter.25
  972.5 60.8 reduce-scatter.27
  1037.7 64.4 reduce-scatter.23
  1104.6 58.1 reduce-scatter.15
where the time goes:
time: 1180 us; the launch traced here: 1170 us
  waiting for transfers between devices  650 us (55%)
  matrix products  250 us (21%)
  blocking collectives  114 us (10%)
  other arithmetic  79.1 us (7%)
  local copies, waits for them, and re-layouts  61.6 us (5%)
  between operations  14.8 us (1%)
    reduce_scatter x2, waiting for transfers between devices, sum_grad_partials(): return lax.psum_scatter(values, 'col', scatter_dimension=1, tiled=True)  117 us
    unnamed x19, waiting for transfers between devices  103 us
    reduce_scatter x3, waiting for transfers between devices, sum_partials(): return lax.psum_scatter(values, 'col', scatter_dimension=1, tiled=True)  99 us
    reduce_scatter x1, waiting for transfers between devices, per_device(): lax.psum_scatter(expand_grad.astype(jnp.bfloat16), 'row', scatter_dimensi...  68 us
    reduce_scatter x1, waiting for transfers between devices, per_device(): lax.psum_scatter(inward_grad.astype(jnp.bfloat16), 'row', scatter_dimensi...  67.1 us
    all_gather x2, waiting for transfers between devices, spread_grads(): return lax.all_gather(values, 'col', axis=1, tiled=True)  60.1 us
    all_gather x3, waiting for transfers between devices, spread_features(): return lax.all_gather(values, 'col', axis=1, tiled=True)  58.9 us
    all_gather x1, waiting for transfers between devices, fetch_weights(): lax.all_gather(reduce_weight, 'row', axis=1, tiled=True)  44.5 us
  transfers between devices with their start and end apart: 17, of which 16 were waited for; matrix products, arithmetic and copies ran while one was open for 12% of the time, Pallas kernels for 0%

commit v1 on v0

--- a/solution.py
+++ b/solution.py
@@ -11,7 +11,9 @@
 
 
 def norm_forward(values, gain, shift, full_width):
-    row_total = lax.psum(jnp.sum(values, axis=1), "col")
+    x = jnp.sum(values, axis=1)
+    parts = lax.all_gather(x, "col")
+    row_total = jnp.sum(parts, axis=0)
     centred = values - (row_total / full_width)[:, None]
     row_square = lax.psum(jnp.sum(centred * centred, axis=1), "col")
     inverse = lax.rsqrt(row_square / full_width + EPSILON)

time: 1180 us -> 1180 us (level)
  waiting for transfers between devices: 650 us -> 637 us
  blocking collectives: 114 us -> 126 us
    unnamed x0 -> x3, blocking collectives: none -> 34.2 us
    psum x3 -> x0, blocking collectives: 25 us -> none  [norm_forward(): row_total = lax.psum(jnp.sum(values, axis=1), 'col')]
  transfers between devices with their start and end apart: 17 -> 17, of which waited for: 16 -> 15; matrix products, arithmetic and copies ran while one was open for 12% -> 12% of each run, Pallas kernels for 0% -> 0%
where the time goes in v1:
time: 1180 us; the launch traced here: 1170 us
  waiting for transfers between devices  637 us (54%)
  matrix products  250 us (21%)
  blocking collectives  126 us (11%)
  other arithmetic  79.1 us (7%)
  local copies, waits for them, and re-layouts  64.6 us (5%)
  between operations  15.5 us (1%)
    reduce_scatter x2, waiting for transfers between devices, sum_grad_partials(): return lax.psum_scatter(values, 'col', scatter_dimension=1, tiled=True)  116 us
    unnamed x19, waiting for transfers between devices  103 us
    reduce_scatter x3, waiting for transfers between devices, sum_partials(): return lax.psum_scatter(values, 'col', scatter_dimension=1, tiled=True)  99.1 us
    reduce_scatter x1, waiting for transfers between devices, per_device(): lax.psum_scatter(expand_grad.astype(jnp.bfloat16), 'row', scatter_dimensi...  68 us
    reduce_scatter x1, waiting for transfers between devices, per_device(): lax.psum_scatter(inward_grad.astype(jnp.bfloat16), 'row', scatter_dimensi...  67.1 us
    all_gather x2, waiting for transfers between devices, spread_grads(): return lax.all_gather(values, 'col', axis=1, tiled=True)  59.7 us
    all_gather x3, waiting for transfers between devices, spread_features(): return lax.all_gather(values, 'col', axis=1, tiled=True)  53.9 us
    all_gather x1, waiting for transfers between devices, fetch_weights(): lax.all_gather(reduce_weight, 'row', axis=1, tiled=True)  44.5 us
  transfers between devices with their start and end apart: 17, of which 15 were waited for; matrix products, arithmetic and copies ran while one was open for 12% of the time, Pallas kernels for 0%

profile of v1, /device:TPU:0, one launch (start us, length us, event | category | flops | bytes accessed | tf_op | source)
XLA Modules:
  0.0 1173.8 jit_solution(4455379884463826610)
XLA Ops:
  11.9 12.8 %all-reduce = f32[6272]{0:T(1024)S(1)} all-reduce(f32[6272]{0:T(1024)S(1)} %dynamic-update-slice), channel_id=2, replica_groups=mesh['row'=8,'col'=4] {'col'}, use_global_device_ids=true, to_apply=%add | all-reduce | flops 6272 | bytes 50176
  25.4 6.2 psum.108
  34.6 33.1 %all_gather.56 = bf16[256,1024]{1,0:T(8,128)(2,1)} all-gather(bf16[256,128]{1,0:T(8,128)(2,1)S(1)} %copy-done.18), channel_id=1, replica_groups=mesh['row'=8,'col'=4] {'row'}, dimensions={1}, use_global_device_ids=true | all-gather | bytes 589824 | tf_op jit(solution)/shard_map/all_gather | solution.py:54
  69.5 24.1 %all-gather.12.cloned.1.call-done = bf16[1568,1024]{1,0:T(8,128)(2,1)} async-done(((bf16[1568,256]{1,0:T(8,128)(2,1)}), bf16[1568,1024]{1,0:T(8,128)(2,1)}) %all-gather.12.cloned.1.call-update) | async-done | bytes 3211280 | tf_op jit(solution)/shard_map/all_gather | solution.py:36
  110.1 34.0 %while.64 = (s32[]{:T(128)}, bf16[2,784,4,64]{1,3,2,0:T(8,128)(2,1)S(1)}, bf16[2,784,4,64]{1,3,2,0:T(8,128)(2,1)}, bf16[1568,4,64]{0,2,1:T(8,128)(2,1)}, bf16[1568,4,64]{0,2,1:T(8,128)(2,1)}, /*index=5*/s32[]{:T(128)}) while((s32[]{:T(128)}, bf16[2,784,4,64]{1,3,2,0:T(8,128)(2,1)S(1)}, bf16[2,784,4,64]{1,3,2,0:T(8,128)(2,1)}, ...), condition=%wide.region_7.0_spmd, body=%wide.region_4.7_spmd.sunk | while | flops 1922650112 | bytes 4304209 | solution.py:78
  110.3 7.7 fusion.207
  118.0 9.0 fusion.208
  127.1 7.7 fusion.207
  134.8 9.0 fusion.208
  150.5 30.1 %while.65 = (s32[]{:T(128)}, bf16[2,784,4,64]{1,3,2,0:T(8,128)(2,1)}, f32[2,4,784]{2,1,0:T(4,128)S(1)}, bf16[2,784,4,64]{1,3,2,0:T(8,128)(2,1)}, bf16[1568,4,64]...) while((s32[]{:T(128)}, bf16[2,784,4,64]{1,3,2,0:T(8,128)(2,1)}, ...), condition=%wide.region_17.18_spmd, body=%wide.region_14.17_spmd.sunk | while | flops 1303067648 | bytes 62078304 | solution.py:78
  158.9 6.7 fusion.212
  174.0 6.6 fusion.212
  189.1 19.6 %reduce-scatter.14.cloned.1.call-done = f32[1568,256]{1,0:T(8,128)} async-done(((f32[1568,1024]{1,0:T(8,128)}), f32[1568,256]{1,0:T(8,128)}) %reduce-scatter.14.cloned.1.call-update) | async-done | bytes 1605648 | tf_op jit(solution)/shard_map/reduce_scatter | solution.py:40
  208.7 61.9 %reduce-scatter.18.cloned.1.call-done = f32[1568,256]{1,0:T(8,128)} async-done(((f32[1568,1024]{1,0:T(8,128)}), f32[1568,256]{1,0:T(8,128)}) %reduce-scatter.18.cloned.1.call-update) | async-done | bytes 1605648 | tf_op jit(solution)/shard_map/reduce_scatter | solution.py:40
  274.9 10.3 all-reduce.2
  285.9 6.7 psum.110
  297.0 25.0 %all-gather.18.cloned.1.call-done = bf16[1024,1024]{1,0:T(8,128)(2,1)} async-done(((bf16[128,1024]{1,0:T(8,128)(2,1)}), bf16[1024,1024]{1,0:T(8,128)(2,1)}) %all-gather.18.cloned.1.call-update) | async-done | bytes 2097168 | tf_op jit(solution)/shard_map/all_gather | solution.py:55
  321.9 29.8 %all-gather.22.cloned.1.call-done = bf16[1568,1024]{1,0:T(8,128)(2,1)} async-done(((bf16[1568,256]{1,0:T(8,128)(2,1)}), bf16[1568,1024]{1,0:T(8,128)(2,1)}) %all-gather.22.cloned.1.call-update) | async-done | bytes 3211280 | tf_op jit(solution)/shard_map/all_gather | solution.py:36
  351.7 8.7 fusion.142
  360.4 44.5 %all-gather.20.cloned.1.call-done = bf16[1024,1024]{1,0:T(8,128)(2,1)} async-done(((bf16[1024,128]{1,0:T(8,128)(2,1)}), bf16[1024,1024]{1,0:T(8,128)(2,1)}) %all-gather.20.cloned.1.call-update) | async-done | bytes 2097168 | tf_op jit(solution)/shard_map/all_gather | solution.py:56
  404.9 29.1 %all-gather.24.cloned.1.call-done = bf16[1568,1024]{1,0:T(8,128)(2,1)} async-done(((bf16[1568,256]{1,0:T(8,128)(2,1)}), bf16[1568,1024]{1,0:T(8,128)(2,1)}) %all-gather.24.cloned.1.call-update) | async-done | bytes 3211280 | tf_op jit(solution)/shard_map/all_gather | solution.py:44
  434.0 22.4 %convert_reduce_fusion = (f32[1024]{0:T(1024)}, bf16[1568,1024]{1,0:T(8,128)(2,1)S(1)}, f32[1568,1024]{1,0:T(8,128)}) fusion(f32[1568,1024]{1,0:T(8,128)} %fusion.142, f32[1024]{0:T(1024)S(1)} %copy-done.34, bf16[1568,1024]{1,0:T(8,128)(2,1)} %all-gather.24.cloned.1.call-done, bf16[1024,1024]{1,0:T(8,128)(2,1)} %all-gather.20.cloned.1.call-done), kind=kOutput, calls=%fused_computation.69 | convolution fusion | flops 3408755712 | bytes 21372928 | tf_op jit(solution)/shard_map/dot_general | solution.py:260
  458.0 5.5 fusion.143
  464.1 58.8 %reduce-scatter.20.cloned.1.call-done = f32[1568,256]{1,0:T(8,128)} async-done(((f32[1568,1024]{1,0:T(8,128)}), f32[1568,256]{1,0:T(8,128)}) %reduce-scatter.20.cloned.1.call-update) | async-done | bytes 1605648 | tf_op jit(solution)/shard_map/reduce_scatter | solution.py:48
  525.9 11.1 all-reduce.5
  541.0 30.6 %all-gather.26.cloned.1.call-done = bf16[1568,1024]{1,0:T(8,128)(2,1)} async-done(((bf16[1568,256]{1,0:T(8,128)(2,1)}), bf16[1568,1024]{1,0:T(8,128)(2,1)}) %all-gather.26.cloned.1.call-update) | async-done | bytes 3211280 | tf_op jit(solution)/shard_map/all_gather | solution.py:44
  579.2 129.4 %while.66 = (s32[]{:T(128)}, f32[1568,4,64]{0,2,1:T(8,128)}, f32[1568,4,64]{0,2,1:T(8,128)}, bf16[2,784,4,64]{1,3,2,0:T(8,128)(2,1)}, bf16[2,784,4,64]{1,3,2,0:T...) while((s32[]{:T(128)}, f32[1568,4,64]{0,2,1:T(8,128)}, ...), condition=%wide.region_30.31_spmd.clone, body=%wide.region_28.30_spmd.clone.sunk | while | flops 3188179968 | bytes 291960320 | solution.py:115
  579.2 11.1 fusion.222
  590.4 13.9 %multiply_reduce_fusion.15 = (f32[4,784]{1,0:T(4,128)S(1)}, f32[4,784,1568]{2,1,0:T(8,128)}) fusion(f32[4,784,1568]{2,1,0:T(8,128)} %fusion.222, f32[4,784]{1,0:T(4,128)S(1)} %dynamic-slice_bitcast_fusion.2, bf16[1568,4,64]{0,2,1:T(8,128)(2,1)} %get-tuple-element.583, bf16[2,784,4,64]{1,3,2,0:T(8,128)(2,1)} %get-tuple-element.582, s32[]{:T(128)S(6)} %copy.125), kind=kOutput, calls=%fused_computation.37.clone.1 | convolution fusion | flops 649073600 | bytes 41878020 | tf_op jit(solution)/shard_map/while/body/eval_jaxpr/while/body/eval_jaxpr/qhd,khd->hqk/dot_general | solution.py:90
  604.2 18.2 %multiply_convert_fusion.6 = bf16[4,784,1568]{2,1,0:T(8,128)(2,1)} fusion(f32[4,784,1568]{2,1,0:T(8,128)} %get-tuple-element.515, f32[4,784,1568]{2,1,0:T(8,128)} %fusion.222, f32[4,784]{1,0:T(4,128)S(1)} %get-tuple-element.516), kind=kLoop, calls=%fused_computation.36.clone.1 | loop fusion | flops 14751744 | bytes 49185024 | tf_op jit(solution)/shard_map/while/body/eval_jaxpr/while/body/eval_jaxpr/convert_element_type | solution.py:98
  631.0 8.3 fusion.225
  643.6 11.1 fusion.222
  654.7 13.9 %multiply_reduce_fusion.15 = (f32[4,784]{1,0:T(4,128)S(1)}, f32[4,784,1568]{2,1,0:T(8,128)}) fusion(f32[4,784,1568]{2,1,0:T(8,128)} %fusion.222, f32[4,784]{1,0:T(4,128)S(1)} %dynamic-slice_bitcast_fusion.2, bf16[1568,4,64]{0,2,1:T(8,128)(2,1)} %get-tuple-element.583, bf16[2,784,4,64]{1,3,2,0:T(8,128)(2,1)} %get-tuple-element.582, s32[]{:T(128)S(6)} %copy.125), kind=kOutput, calls=%fused_computation.37.clone.1 | convolution fusion | flops 649073600 | bytes 41878020 | tf_op jit(solution)/shard_map/while/body/eval_jaxpr/while/body/eval_jaxpr/qhd,khd->hqk/dot_general | solution.py:90
  668.6 18.2 %multiply_convert_fusion.6 = bf16[4,784,1568]{2,1,0:T(8,128)(2,1)} fusion(f32[4,784,1568]{2,1,0:T(8,128)} %get-tuple-element.515, f32[4,784,1568]{2,1,0:T(8,128)} %fusion.222, f32[4,784]{1,0:T(4,128)S(1)} %get-tuple-element.516), kind=kLoop, calls=%fused_computation.36.clone.1 | loop fusion | flops 14751744 | bytes 49185024 | tf_op jit(solution)/shard_map/while/body/eval_jaxpr/while/body/eval_jaxpr/convert_element_type | solution.py:98
  696.0 8.3 fusion.225
  719.3 6.0 convolution_bitcast_fusion.1
  727.2 57.5 %reduce-scatter.22.cloned.1.call-done = f32[1568,256]{1,0:T(8,128)} async-done(((f32[1568,1024]{1,0:T(8,128)}), f32[1568,256]{1,0:T(8,128)}) %reduce-scatter.22.cloned.1.call-update) | async-done | bytes 1605648 | tf_op jit(solution)/shard_map/reduce_scatter | solution.py:48
  787.1 10.3 all-reduce.4
  798.9 11.4 fusion.95
  814.8 8.3 convolution_convert_fusion.1
  829.4 6.9 fusion.96
  836.6 23.6 %fusion.94 = f32[1568,1024]{1,0:T(8,128)} fusion(bf16[1024,1024]{1,0:T(8,128)(2,1)} %all-gather.20.cloned.1.call-done, bf16[1568,1024]{1,0:T(8,128)(2,1)} %all-gather.16.cloned.1.call-done, bf16[1024,1024]{1,0:T(8,128)(2,1)} %all-gather.18.cloned.1.call-done, f32[1024]{0:T(1024)S(1)} %copy-done.35), kind=kOutput, calls=%fused_computation.110 | convolution fusion | flops 6682640384 | bytes 13832192 | tf_op jit(solution)/shard_map/dot_general | solution.py:171
  860.2 40.4 %reduce-scatter.30.cloned.1.call-done = bf16[128,1024]{1,0:T(8,128)(2,1)} async-done(((bf16[1024,1024]{1,0:T(8,128)(2,1)}), bf16[128,1024]{1,0:T(8,128)(2,1)}) %reduce-scatter.30.cloned.1.call-update) | async-done | bytes 262160
  902.7 68.0 %reduce-scatter.26.cloned.1.call-done = bf16[128,1024]{1,0:T(8,128)(2,1)} async-done(((bf16[1024,1024]{1,0:T(8,128)(2,1)}), bf16[128,1024]{1,0:T(8,128)(2,1)}) %reduce-scatter.26.cloned.1.call-update) | async-done | bytes 262160 | tf_op jit(solution)/shard_map/reduce_scatter | solution.py:342
  974.1 60.7 %reduce-scatter.28.cloned.1.call-done = bf16[128,256]{1,0:T(8,128)(2,1)} async-done(((bf16[1024,256]{1,0:T(8,128)(2,1)}), bf16[128,256]{1,0:T(8,128)(2,1)}) %reduce-scatter.28.cloned.1.call-update) | async-done | bytes 65552
  1036.4 67.1 %reduce-scatter.24.cloned.1.call-done = bf16[128,3,256]{2,0,1:T(8,128)(2,1)} async-done(((bf16[1024,3,256]{2,0,1:T(8,128)(2,1)}), bf16[128,3,256]{2,0,1:T(8,128)(2,1)}) %reduce-scatter.24.cloned.1.call-update) | async-done | bytes 196624 | tf_op jit(solution)/shard_map/reduce_scatter | solution.py:336
  1111.5 35.2 %all-reduce.3 = (f32[256]{0:T(256)}, f32[256]{0:T(256)}, f32[2,256]{1,0:T(2,128)}, f32[256]{0:T(256)}, f32[256]{0:T(256)}, /*index=5*/f32[256]{0:T(256)}, f32[1024]{0:T(1024)}, f32[256]{0:T(256)}) all-reduce(f32[256]{0:T(256)S(1)} %get-tuple-element.301, f32[256]{0:T(256)S(1)} %get-tuple-element.308, ...), channel_id=1, replica_groups=mesh['row'=8,'col'=4] {'row'}, use_global_device_ids=true, to_apply=%region_37.38 | all-reduce | flops 3072 | bytes 24576 | tf_op jit(solution)/shard_map/psum | solution.py:358
  1146.7 17.6 %reduce-scatter.16.cloned.1.call-done = f32[1568,256]{1,0:T(8,128)} async-done(((f32[1568,1024]{1,0:T(8,128)}), f32[1568,256]{1,0:T(8,128)}) %reduce-scatter.16.cloned.1.call-update) | async-done | bytes 1605648 | tf_op jit(solution)/shard_map/reduce_scatter | solution.py:40
  (215 shorter events, 154.9 us)
Async XLA Ops:
  7.2 27.3 %copy-start.30 = (f32[2,256]{1,0:T(2,128)S(1)}, f32[2,256]{1,0:T(2,128)}, u32[]{:S(2)}) copy-start(f32[2,256]{1,0:T(2,128)} %param.24) | copy-start | bytes 6148
  7.2 27.4 %copy-start.18 = (bf16[256,128]{1,0:T(8,128)(2,1)S(1)}, bf16[256,128]{1,0:T(8,128)(2,1)}, u32[]{:S(2)}) copy-start(bf16[256,128]{1,0:T(8,128)(2,1)} %param.25) | copy-start | bytes 196612
  7.2 60.5 %all-gather.14.cloned.1.call-start = ((), (), s32[]{:S(2)}) async-start(), calls=%async_computation.10 | async-start | bytes 1769472 | tf_op jit(solution)/shard_map/all_gather | solution.py:53
  7.9 85.6 %all-gather.12.cloned.1.call-start = ((), (), s32[]{:S(2)}) async-start(), calls=%async_computation.9 | async-start | bytes 4014080 | tf_op jit(solution)/shard_map/all_gather | solution.py:36
  9.3 88.8 %copy-start.2 = (f32[1568,256]{1,0:T(8,128)}, f32[1568,256]{1,0:T(8,128)S(1)}, u32[]{:S(2)}) copy-start(f32[1568,256]{1,0:T(8,128)S(1)} %reshape.171) | copy-start | bytes 4816900
  24.9 42.9 %copy-start.14 = (f32[1568]{0:T(1024)}, f32[1568]{0:T(1024)S(1)}, u32[]{:S(2)}) copy-start(f32[1568]{0:T(1024)S(1)} %broadcast_multiply_fusion.7) | copy-start | bytes 18820
  34.4 174.4 %reduce-scatter.14.cloned.1.call-start = ((), (), s32[]{:S(2)}) async-start(), calls=%async_computation.11 | async-start | bytes 8028160 | tf_op jit(solution)/shard_map/reduce_scatter | solution.py:40
  110.1 35.5 %copy-start.12 = (bf16[256,1024]{1,0:T(8,128)(2,1)S(1)}, bf16[256,1024]{1,0:T(8,128)(2,1)}, u32[]{:S(2)}) copy-start(bf16[256,1024]{1,0:T(8,128)(2,1)} %all_gather.56) | copy-start | bytes 1572868
  149.4 121.3 %reduce-scatter.18.cloned.1.call-start = ((), (), s32[]{:S(2)}) async-start(), calls=%async_computation.16 | async-start | bytes 8028160 | tf_op jit(solution)/shard_map/reduce_scatter | solution.py:40
  183.3 87.3 %copy-start.3 = (f32[1568,256]{1,0:T(8,128)S(1)}, f32[1568,256]{1,0:T(8,128)}, u32[]{:S(2)}) copy-start(f32[1568,256]{1,0:T(8,128)} %copy-done.2) | copy-start | bytes 4816900
  183.3 87.3 %copy-start.31 = (f32[256]{0:T(256)S(1)}, f32[256]{0:T(256)}, u32[]{:S(2)}) copy-start(f32[256]{0:T(256)} %param.26) | copy-start | bytes 3076
  188.5 104.1 %copy-start.20 = (f32[256]{0:T(256)S(1)}, f32[256]{0:T(256)}, u32[]{:S(2)}) copy-start(f32[256]{0:T(256)} %param.27) | copy-start | bytes 3076
  188.5 104.1 %copy-start.23 = (f32[256]{0:T(256)S(1)}, f32[256]{0:T(256)}, u32[]{:S(2)}) copy-start(f32[256]{0:T(256)} %param.28) | copy-start | bytes 3076
  188.5 133.4 %all-gather.18.cloned.1.call-start = ((), (), s32[]{:S(2)}) async-start(), calls=%async_computation.13 | async-start | bytes 2359296 | tf_op jit(solution)/shard_map/all_gather | solution.py:55
  189.1 162.6 %all-gather.22.cloned.1.call-start = ((), (), s32[]{:S(2)}) async-start(), calls=%async_computation.17 | async-start | bytes 4014080 | tf_op jit(solution)/shard_map/all_gather | solution.py:36
  294.0 110.9 %all-gather.20.cloned.1.call-start = ((), (), s32[]{:S(2)}) async-start(), calls=%async_computation.14 | async-start | bytes 2359296 | tf_op jit(solution)/shard_map/all_gather | solution.py:56
  294.7 139.2 %all-gather.24.cloned.1.call-start = ((), (), s32[]{:S(2)}) async-start(), calls=%async_computation.18 | async-start | bytes 4014080 | tf_op jit(solution)/shard_map/all_gather | solution.py:44
  296.9 137.1 %copy-start.34 = (f32[1024]{0:T(1024)S(1)}, f32[1024]{0:T(1024)}, u32[]{:S(2)}) copy-start(f32[1024]{0:T(1024)} %param.30) | copy-start | bytes 12292
  296.9 226.0 %reduce-scatter.20.cloned.1.call-start = ((), (), s32[]{:S(2)}) async-start(), calls=%async_computation.19 | async-start | bytes 8028160 | tf_op jit(solution)/shard_map/reduce_scatter | solution.py:48
  434.0 24.1 %copy-start.33 = (bf16[1024,1024]{1,0:T(8,128)(2,1)S(1)}, bf16[1024,1024]{1,0:T(8,128)(2,1)}, u32[]{:S(2)}) copy-start(bf16[1024,1024]{1,0:T(8,128)(2,1)} %all-gather.18.cloned.1.call-done) | copy-start | bytes 6291460
  463.5 73.5 %copy-start.9 = (bf16[1568,256]{1,0:T(8,128)(2,1)S(1)}, bf16[1568,256]{1,0:T(8,128)(2,1)}, u32[]{:S(2)}) copy-start(bf16[1568,256]{1,0:T(8,128)(2,1)} %reshape.168) | copy-start | bytes 2408452
  463.6 108.0 %copy-start.13 = (bf16[256,1024]{1,0:T(8,128)(2,1)S(1)}, bf16[256,1024]{1,0:T(8,128)(2,1)}, u32[]{:S(2)}) copy-start(bf16[256,1024]{1,0:T(8,128)(2,1)} %all_gather.56) | copy-start | bytes 1572868
  463.6 108.0 %all-gather.26.cloned.1.call-start = ((), (), s32[]{:S(2)}) async-start(), calls=%async_computation.20 | async-start | bytes 4014080 | tf_op jit(solution)/shard_map/all_gather | solution.py:44
  540.9 243.8 %reduce-scatter.22.cloned.1.call-start = ((), (), s32[]{:S(2)}) async-start(), calls=%async_computation.21 | async-start | bytes 8028160 | tf_op jit(solution)/shard_map/reduce_scatter | solution.py:48
  604.2 22.7 %copy-start = (f32[4,784,1568]{2,1,0:T(8,128)S(1)}, f32[4,784,1568]{2,1,0:T(8,128)}, u32[]{:S(2)}) copy-start(f32[4,784,1568]{2,1,0:T(8,128)} %get-tuple-element.515) | copy-start | bytes 59006980 | tf_op jit(solution)/shard_map/while/body/eval_jaxpr/while
  631.0 8.3 copy-start.1
  631.0 8.3 copy-start.5
  668.6 22.7 %copy-start = (f32[4,784,1568]{2,1,0:T(8,128)S(1)}, f32[4,784,1568]{2,1,0:T(8,128)}, u32[]{:S(2)}) copy-start(f32[4,784,1568]{2,1,0:T(8,128)} %get-tuple-element.515) | copy-start | bytes 59006980 | tf_op jit(solution)/shard_map/while/body/eval_jaxpr/while
  696.0 8.3 copy-start.5
  725.3 59.5 %copy-start.4 = (f32[1568,256]{1,0:T(8,128)S(1)}, f32[1568,256]{1,0:T(8,128)}, u32[]{:S(2)}) copy-start(f32[1568,256]{1,0:T(8,128)} %copy-done.2) | copy-start | bytes 4816900
  725.3 59.5 %copy-start.15 = (f32[1568]{0:T(1024)S(1)}, f32[1568]{0:T(1024)}, u32[]{:S(2)}) copy-start(f32[1568]{0:T(1024)} %copy-done.14) | copy-start | bytes 18820
  725.3 59.5 %copy-start.17 = (f32[1568]{0:T(1024)S(1)}, f32[1568]{0:T(1024)}, u32[]{:S(2)}) copy-start(f32[1568]{0:T(1024)} %copy-done.16) | copy-start | bytes 18820
  725.3 59.5 %copy-start.22 = (f32[256]{0:T(256)S(1)}, f32[256]{0:T(256)}, u32[]{:S(2)}) copy-start(f32[256]{0:T(256)} %param.21) | copy-start | bytes 3076
  725.3 72.1 %copy-start.21 = (f32[256]{0:T(256)S(1)}, f32[256]{0:T(256)}, u32[]{:S(2)}) copy-start(f32[256]{0:T(256)} %param.27) | copy-start | bytes 3076
  725.3 72.1 %copy-start.24 = (f32[256]{0:T(256)S(1)}, f32[256]{0:T(256)}, u32[]{:S(2)}) copy-start(f32[256]{0:T(256)} %param.28) | copy-start | bytes 3076
  725.3 73.6 %copy-start.35 = (f32[1024]{0:T(1024)S(1)}, f32[1024]{0:T(1024)}, u32[]{:S(2)}) copy-start(f32[1024]{0:T(1024)} %param.30) | copy-start | bytes 12292
  725.4 111.2 %all-gather.16.cloned.1.call-start = ((), (), s32[]{:S(2)}) async-start(), calls=%async_computation.12 | async-start | bytes 4014080 | tf_op jit(solution)/shard_map/all_gather | solution.py:36
  798.8 101.8 %reduce-scatter.30.cloned.1.call-start = ((), (), s32[]{:S(2)}) async-start(), calls=%async_computation.25 | async-start | bytes 2359296
  814.3 156.3 %reduce-scatter.26.cloned.1.call-start = ((), (), s32[]{:S(2)}) async-start(), calls=%async_computation.23 | async-start | bytes 2359296 | tf_op jit(solution)/shard_map/reduce_scatter | solution.py:342
  823.1 211.7 %reduce-scatter.28.cloned.1.call-start = ((), (), s32[]{:S(2)}) async-start(), calls=%async_computation.24 | async-start | bytes 589824
  829.4 274.2 %reduce-scatter.24.cloned.1.call-start = ((), (), s32[]{:S(2)}) async-start(), calls=%async_computation.22 | async-start | bytes 1769472 | tf_op jit(solution)/shard_map/reduce_scatter | solution.py:336
  836.3 327.9 %reduce-scatter.16.cloned.1.call-start = ((), (), s32[]{:S(2)}) async-start(), calls=%async_computation.15 | async-start | bytes 8028160 | tf_op jit(solution)/shard_map/reduce_scatter | solution.py:40
  902.6 208.8 %copy-start.25 = (f32[256]{0:T(256)S(1)}, f32[256]{0:T(256)}, u32[]{:S(2)}) copy-start(f32[256]{0:T(256)} %get-tuple-element.299) | copy-start | bytes 3076
  902.6 208.8 %copy-start.26 = (f32[256]{0:T(256)S(1)}, f32[256]{0:T(256)}, u32[]{:S(2)}) copy-start(f32[256]{0:T(256)} %get-tuple-element.307) | copy-start | bytes 3076
  902.6 208.8 %copy-start.27 = (f32[256]{0:T(256)S(1)}, f32[256]{0:T(256)}, u32[]{:S(2)}) copy-start(f32[256]{0:T(256)} %get-tuple-element.368) | copy-start | bytes 3076
  902.6 208.8 %copy-start.28 = (f32[256]{0:T(256)S(1)}, f32[256]{0:T(256)}, u32[]{:S(2)}) copy-start(f32[256]{0:T(256)} %get-tuple-element.383) | copy-start | bytes 3076
  902.6 208.8 %copy-start.29 = (f32[1024]{0:T(1024)S(1)}, f32[1024]{0:T(1024)}, u32[]{:S(2)}) copy-start(f32[1024]{0:T(1024)} %get-tuple-element.365) | copy-start | bytes 12292
  902.6 261.6 %copy-start.32 = (f32[256]{0:T(256)S(1)}, f32[256]{0:T(256)}, u32[]{:S(2)}) copy-start(f32[256]{0:T(256)} %param.32) | copy-start | bytes 3076
  (10 other events, 28.9 us)
Sparse Core Ops, SparseCore 0:
  10.2 50.4 all-gather.13
  62.9 30.5 all-gather.11
  149.5 59.2 reduce-scatter.13
  211.3 59.2 reduce-scatter.17
  272.6 49.2 all-gather.17
  323.9 27.7 all-gather.21
  353.8 51.0 all-gather.19
  406.4 27.4 all-gather.23
  463.7 59.2 reduce-scatter.19
  541.0 30.4 all-gather.25
  725.5 59.2 reduce-scatter.21
  798.9 30.3 all-gather.15
  832.9 67.7 reduce-scatter.29
  904.1 66.5 reduce-scatter.25
  973.8 60.9 reduce-scatter.27
  1039.1 64.4 reduce-scatter.23
  1106.0 58.2 reduce-scatter.15
